TPU v7x, 256 devices: a whole 4x4x8 slice. The times are simulated.
256 devices in a mesh: date: 64 (over x_hi, z, y), rng: 4 (over x_lo, core).
Axes of the slice: x: 4 (x_hi: 2, x_lo: 2; x = x_hi * 2 + x_lo), y: 4, z: 8, core: 2. Of those that a mesh axis runs over, the one named last changes fastest.
Arguments:
- slc: bfloat16 [64, 2, 64, 4096], P('date', None, None, 'rng'), may hold values from -9 to 9
- ref_date: int32 [1], replicated, may hold values from 0 to 63
- int_offset: int32 [64, 1, 64], P('date', None, 'rng'), may hold values from -4 to 4
- frac_offset: float32 [64, 1, 64], P('date', None, 'rng'), may hold values from 0 to 1
- partners: int32 [64, 4], P('date'), may hold values from 0 to 1, as said below
Outputs:
- surface: float32 [64, 1, 64, 1024], P('date', None, 'rng')
- coherence: bfloat16 [64, 4, 64, 4096], P('date', None, None, 'rng')
Inputs may be any that keep to these rules, and one draw needn't show every extreme that they name: `partners`: each row holds 2 to 4 ones.
All inputs are finite; a program needn't handle non-finite values.
Results may differ from a plain program's by a relative error of at most 0.009.
Values may be sent and summed in bfloat16 or wider, within the bound.
A program may use at most 64 MiB of HBM per device.

v0:
```python
import jax
import jax.numpy as jnp
from jax import lax
from jax.sharding import PartitionSpec as P

BLK = 64
OVS = 2
LAGS = 32
IMAX = 4
SPAN = 4
BOXA = 5
BOXR = 19


HIGHEST = lax.Precision.HIGHEST


def from_root(value, axis, root):
    mine = lax.axis_index(axis) == root
    return lax.psum(jnp.where(mine, value, jnp.zeros_like(value)), axis)


def with_halo(value, sides, width):
    for axis, dim in sides:
        devices, length = (lax.axis_size(axis), value.shape[dim])
        up = [(i, (i + 1) % devices) for i in range(devices - 1)]
        down = [(j, i) for i, j in up]
        last = lax.slice_in_dim(value, length - width, length, axis=dim)
        leading = lax.slice_in_dim(value, 0, width, axis=dim)
        before = lax.ppermute(last, axis, up)
        after = lax.ppermute(leading, axis, down)
        value = jnp.concatenate([before, value, after], axis=dim)
    return value


def passed_along(value, axis, steps):
    count = lax.axis_size(axis)
    leading, last = (max(0, -steps), min(count, count - steps))
    return lax.ppermute(value, axis, [(source, source + steps) for source in range(leading, last)])


def dft_tables(block, lags, factor):
    index = jnp.arange(block, dtype=jnp.int32)
    phase = index[:, None] * index[None, :] % block
    angle = 2.0 * jnp.pi / block * phase.astype(jnp.float32)
    upsampled = factor * block
    signed = jnp.where(index < block // 2, index, index - block)
    lag_index = jnp.arange(lags, dtype=jnp.int32) - lags // 2
    lag_phase = lag_index[:, None] * signed[None, :] % upsampled
    lag_angle = 2.0 * jnp.pi / upsampled * lag_phase.astype(jnp.float32)
    return (jnp.cos(angle), jnp.sin(angle), jnp.cos(lag_angle), jnp.sin(lag_angle))


def amplitude(slab):
    real_part = slab[0].astype(jnp.float32)
    imag_part = slab[1].astype(jnp.float32)
    return jnp.sqrt(real_part * real_part + imag_part * imag_part + 1e-06).astype(jnp.bfloat16)


def prepare(amplitude_map, block):
    rows, cols = amplitude_map.shape
    blocks = amplitude_map.astype(jnp.float32).reshape(rows // block, block, cols // block, block)
    blocks = blocks.transpose(0, 2, 1, 3)
    centered = blocks - jnp.mean(blocks, axis=(2, 3), keepdims=True)
    energy = jnp.sum(centered * centered, axis=(2, 3))
    return (centered, energy)


def spectra(centered, cosine, sine):
    first_real = jnp.einsum("kn,abnm->abkm", cosine, centered, precision=HIGHEST)
    first_imag = -jnp.einsum("kn,abnm->abkm", sine, centered, precision=HIGHEST)
    real_part = jnp.einsum("abkn,ln->abkl", first_real, cosine, precision=HIGHEST) + jnp.einsum(
        "abkn,ln->abkl", first_imag, sine, precision=HIGHEST
    )
    imag_part = jnp.einsum("abkn,ln->abkl", first_imag, cosine, precision=HIGHEST) - jnp.einsum(
        "abkn,ln->abkl", first_real, sine, precision=HIGHEST
    )
    return (real_part, imag_part)


def correlate(own_amplitude, ref_amplitude):
    cosine, sine, lag_cos, lag_sin = dft_tables(BLK, LAGS, OVS)
    own_blocks, own_energy = prepare(own_amplitude, BLK)
    ref_blocks, ref_energy = prepare(ref_amplitude, BLK)
    own_real, own_imag = spectra(own_blocks, cosine, sine)
    ref_real, ref_imag = spectra(ref_blocks, cosine, sine)
    cross_real = own_real * ref_real + own_imag * ref_imag
    cross_imag = own_imag * ref_real - own_real * ref_imag
    left_real = jnp.einsum("mk,abkl->abml", lag_cos, cross_real, precision=HIGHEST) - jnp.einsum(
        "mk,abkl->abml", lag_sin, cross_imag, precision=HIGHEST
    )
    left_imag = jnp.einsum("mk,abkl->abml", lag_cos, cross_imag, precision=HIGHEST) + jnp.einsum(
        "mk,abkl->abml", lag_sin, cross_real, precision=HIGHEST
    )
    values = jnp.einsum("abml,nl->abmn", left_real, lag_cos, precision=HIGHEST) - jnp.einsum(
        "abml,nl->abmn", left_imag, lag_sin, precision=HIGHEST
    )
    scale = BLK * jnp.sqrt(own_energy * ref_energy + 1e-06)
    values = values / scale[:, :, None, None]
    return values.reshape(values.shape[0], values.shape[1], LAGS * LAGS)


def resample(padded, shifts, fractions, block, rim):
    block_rows, block_cols = shifts.shape
    row_start = jnp.broadcast_to(
        (jnp.arange(block_rows, dtype=jnp.int32) * block)[:, None], (block_rows, block_cols)
    ).reshape(-1)
    col_start = (
        (jnp.arange(block_cols, dtype=jnp.int32) * block)[None, :] + shifts + (rim - 3)
    ).reshape(-1)
    anchor = jnp.zeros((), jnp.int32)

    def tile(row, col):
        return lax.dynamic_slice(padded, (anchor, row, col), (2, block, block + 7))

    tiles = jax.vmap(tile)(row_start, col_start)
    distance = jnp.arange(8, dtype=jnp.float32)[None, :] - 3.0 - fractions.reshape(-1)[:, None]
    weights = jnp.sinc(distance) * (0.5 + 0.5 * jnp.cos(jnp.pi * distance / 4.0))
    result = weights[:, 0, None, None, None] * tiles[..., 0:block].astype(jnp.float32)
    for tap in range(1, 8):
        result = result + weights[:, tap, None, None, None] * tiles[..., tap : tap + block].astype(
            jnp.float32
        )
    result = result.reshape(block_rows, block_cols, 2, block, block).transpose(2, 0, 3, 1, 4)
    return result.reshape(2, block_rows * block, block_cols * block).astype(jnp.bfloat16)


def boxcar(field, box_rows, box_cols):
    half = box_rows // 2
    padded = jnp.pad(field, ((half, half), (0, 0)))
    rows = field.shape[0]
    summed = padded[0:rows]
    for offset in range(1, box_rows):
        summed = summed + padded[offset : offset + rows]
    width = field.shape[1] - (box_cols - 1)
    total = summed[:, 0:width]
    for offset in range(1, box_cols):
        total = total + summed[:, offset : offset + width]
    return total


def own_fields(own_ext):
    own_real = own_ext[0].astype(jnp.float32)
    own_imag = own_ext[1].astype(jnp.float32)
    box_own = boxcar(own_real * own_real + own_imag * own_imag, BOXA, BOXR)
    return (own_real, own_imag, box_own)


def coherence_pair(own_real, own_imag, box_own, partner_ext, weight):
    other_real = partner_ext[0].astype(jnp.float32)
    other_imag = partner_ext[1].astype(jnp.float32)
    box_re = boxcar(own_real * other_real + own_imag * other_imag, BOXA, BOXR)
    box_im = boxcar(own_imag * other_real - own_real * other_imag, BOXA, BOXR)
    box_partner = boxcar(other_real * other_real + other_imag * other_imag, BOXA, BOXR)
    value = (
        weight.astype(jnp.float32)
        * (box_re * box_re + box_im * box_im)
        / (box_own * box_partner + 1e-06)
    )
    return value.astype(jnp.bfloat16)


def body(slc, ref_date, int_offset, frac_offset, partners):
    own = slc[0]
    own_amplitude = amplitude(own)
    ref_slab = from_root(own, "date", ref_date[0])
    ref_amplitude = amplitude(ref_slab)
    surface = correlate(own_amplitude, ref_amplitude)[None]
    rim = IMAX + 4
    padded = with_halo(own, (("rng", 2),), rim)
    resampled = resample(padded, int_offset[0], frac_offset[0], BLK, rim)
    extended = with_halo(resampled, (("rng", 2),), BOXR // 2)
    own_real, own_imag, box_own = own_fields(extended)
    results = []
    for ahead in range(1, SPAN + 1):
        partner = passed_along(extended, "date", -ahead)
        results.append(coherence_pair(own_real, own_imag, box_own, partner, partners[0, ahead - 1]))
    return (surface, jnp.stack(results)[None])


def solution(mesh):
    in_specs = (
        P("date", None, None, "rng"),
        P(),
        P("date", None, "rng"),
        P("date", None, "rng"),
        P("date", None),
    )
    out_specs = (P("date", None, "rng", None), P("date", None, None, "rng"))
    return jax.shard_map(body, mesh=mesh, in_specs=in_specs, out_specs=out_specs, check_vma=False)
```

profile of v0, /device:TPU:24, one launch (start us, length us, event | category | flops | bytes accessed | tf_op | source)
XLA Modules:
  0.0 701.6 jit_solution(5116876738006215532)
XLA Ops:
  7.9 1.7 broadcast_select_fusion
  9.5 0.9 copy-done
  10.6 1.7 collective-permute-start
  12.3 1.3 collective-permute-start.1
  14.1 0.7 fusion.1
  14.9 0.7 convolution_bitcast_fusion.1
  15.6 1.0 fusion.147
  16.6 1.0 fusion.152
  17.6 1.0 convolution_subtract_fusion.1
  19.5 0.7 fusion.297
  20.5 1.0 copy.62
  21.4 1.7 gather_fusion
  23.2 4.5 fusion.294
  27.6 2.0 copy.89
  29.6 2.0 copy.88
  31.6 1.1 copy.87
  32.7 2.0 copy.86
  34.7 1.1 copy.85
  35.8 2.0 copy.84
  37.8 1.1 copy.83
  38.8 1.1 copy.82
  39.9 2.9 fusion.11
  43.6 4.3 collective-permute-start.2
  47.9 1.3 collective-permute-start.3
  52.6 2.1 collective-permute-start.6
  54.7 1.9 collective-permute-start.4
  56.6 2.7 collective-permute-start.5
  59.4 10.0 %collective-permute-start.7 = (bf16[2,64,1042]{2,1,0:T(8,128)(2,1)S(1)}, bf16[2,64,1042]{2,1,0:T(8,128)(2,1)}, u32[]{:S(2)}, u32[]{:S(2)}) collective-permute-start(bf16[2,64,1042]{2,1,0:T(8,128)(2,1)S(1)} %concatenate.12), channel_id=1, source_target_pairs={{16,0},{20,4},{24,8},{28,12},{32,16},{36,20},{40,24},{44,28},{48,3... | collective-permute-start | bytes 800264 | tf_op jit(solution)/shard_map/ppermute | solution.py:39
  69.4 587.3 %all-reduce.16.cloned.1.call-done = bf16[2,64,1024]{2,1,0:T(8,128)(2,1)} async-done(((bf16[2,64,1024]{2,1,0:T(8,128)(2,1)}), bf16[2,64,1024]{2,1,0:T(8,128)(2,1)}) %all-reduce.16.cloned.1.call-update) | async-done | bytes 262160 | tf_op jit(solution)/shard_map/psum | solution.py:20
  656.7 1.8 fusion.292
  658.5 1.1 copy.81
  659.8 0.7 fusion
  660.6 0.7 convolution_bitcast_fusion
  661.7 1.0 fusion.145
  662.7 1.0 fusion.149
  663.7 1.0 convolution_subtract_fusion
  664.7 1.0 convolution_add_fusion
  665.8 1.0 multiply_subtract_fusion
  670.1 0.8 broadcast_in_dim_reshape.3
  670.9 1.3 fusion.83
  672.5 1.0 fusion.71
  673.7 1.2 fusion.87
  674.9 1.0 fusion.69
  677.4 5.0 fusion.135
  682.4 3.7 fusion.132
  686.1 3.7 fusion.133
  689.8 3.7 fusion.134
  693.5 0.9 maximum_bitcast_fusion
  (62 shorter events, 9.0 us)
Async XLA Ops:
  7.2 649.5 %all-reduce.16.cloned.1.call-start = ((), (), s32[]{:S(2)}) async-start(), calls=%async_computation | async-start | bytes 524288 | tf_op jit(solution)/shard_map/psum | solution.py:20
  9.5 0.9 copy-start
  10.6 9.6 %collective-permute-start = (bf16[2,64,8]{2,1,0:T(8,128)(2,1)S(1)}, bf16[2,64,8]{2,1,0:T(8,128)(2,1)S(1)}, u32[]{:S(2)}, u32[]{:S(2)}) collective-permute-start(bf16[2,64,8]{2,1,0:T(8,128)(2,1)S(1)} %get-tuple-element.31), channel_id=1, source_target_pairs={{0,1},{1,2},{2,3},{4,5},{5,6},{6,7},{8,9},{9,10},{10,11},{12,13},{... | collective-permute-start | bytes 6152 | tf_op jit(solution)/shard_map/ppermute | solution.py:30
  12.3 7.9 %collective-permute-start.1 = (bf16[2,64,8]{2,1,0:T(8,128)(2,1)S(1)}, bf16[2,64,8]{2,1,0:T(8,128)(2,1)S(1)}, u32[]{:S(2)}, u32[]{:S(2)}) collective-permute-start(bf16[2,64,8]{2,1,0:T(8,128)(2,1)S(1)} %get-tuple-element.30), channel_id=1, source_target_pairs={{1,0},{2,1},{3,2},{5,4},{6,5},{7,6},{9,8},{10,9},{11,10},{13,12},{... | collective-permute-start | bytes 6152 | tf_op jit(solution)/shard_map/ppermute | solution.py:31
  17.6 1.0 copy-start.7
  17.6 1.8 copy-start.5
  18.7 0.7 copy-start.6
  29.6 2.0 copy-start.3
  32.7 2.0 copy-start.2
  35.8 2.0 copy-start.1
  38.8 1.1 copy-start.4
  43.6 8.1 %collective-permute-start.2 = (bf16[2,64,9]{2,1,0:T(8,128)(2,1)S(1)}, bf16[2,64,9]{2,1,0:T(8,128)(2,1)S(1)}, u32[]{:S(2)}, u32[]{:S(2)}) collective-permute-start(bf16[2,64,9]{2,1,0:T(8,128)(2,1)S(1)} %get-tuple-element.29), channel_id=1, source_target_pairs={{0,1},{1,2},{2,3},{4,5},{5,6},{6,7},{8,9},{9,10},{10,11},{12,13},{... | collective-permute-start | bytes 6920 | tf_op jit(solution)/shard_map/ppermute | solution.py:30
  47.9 4.4 collective-permute-start.3
  52.6 619.8 %collective-permute-start.6 = (bf16[2,64,1042]{2,1,0:T(8,128)(2,1)S(1)}, bf16[2,64,1042]{2,1,0:T(8,128)(2,1)S(1)}, u32[]{:S(2)}, u32[]{:S(2)}) collective-permute-start(bf16[2,64,1042]{2,1,0:T(8,128)(2,1)S(1)} %concatenate.12), channel_id=1, source_target_pairs={{12,0},{16,4},{20,8},{24,12},{28,16},{32,20},{36,24},{40,28},{44,3... | collective-permute-start | bytes 800264 | tf_op jit(solution)/shard_map/ppermute | solution.py:39
  54.7 619.0 %collective-permute-start.4 = (bf16[2,64,1042]{2,1,0:T(8,128)(2,1)S(1)}, bf16[2,64,1042]{2,1,0:T(8,128)(2,1)}, u32[]{:S(2)}, u32[]{:S(2)}) collective-permute-start(bf16[2,64,1042]{2,1,0:T(8,128)(2,1)S(1)} %concatenate.12), channel_id=1, source_target_pairs={{4,0},{8,4},{12,8},{16,12},{20,16},{24,20},{28,24},{32,28},{36,32}... | collective-permute-start | bytes 800264 | tf_op jit(solution)/shard_map/ppermute | solution.py:39
  56.6 614.2 %collective-permute-start.5 = (bf16[2,64,1042]{2,1,0:T(8,128)(2,1)S(1)}, bf16[2,64,1042]{2,1,0:T(8,128)(2,1)}, u32[]{:S(2)}, u32[]{:S(2)}) collective-permute-start(bf16[2,64,1042]{2,1,0:T(8,128)(2,1)S(1)} %concatenate.12), channel_id=1, source_target_pairs={{8,0},{12,4},{16,8},{20,12},{24,16},{28,20},{32,24},{36,28},{40,32... | collective-permute-start | bytes 800264 | tf_op jit(solution)/shard_map/ppermute | solution.py:39
  59.4 611.5 %collective-permute-start.7 = (bf16[2,64,1042]{2,1,0:T(8,128)(2,1)S(1)}, bf16[2,64,1042]{2,1,0:T(8,128)(2,1)}, u32[]{:S(2)}, u32[]{:S(2)}) collective-permute-start(bf16[2,64,1042]{2,1,0:T(8,128)(2,1)S(1)} %concatenate.12), channel_id=1, source_target_pairs={{16,0},{20,4},{24,8},{28,12},{32,16},{36,20},{40,24},{44,28},{48,3... | collective-permute-start | bytes 800264 | tf_op jit(solution)/shard_map/ppermute | solution.py:39
Sparse Core Ops, SparseCore 0:
  10.6 646.0 all-reduce.15
where the time goes:
time: 715 us; the launch traced here: 702 us
  waiting for transfers between devices  588 us (82%)
  other arithmetic  30.7 us (4%)
  starting transfers between devices  25.4 us (4%)
  local copies, waits for them, and re-layouts  25.3 us (4%)
  between operations  18.1 us (3%)
  matrix products  14.2 us (2%)
    psum x1, waiting for transfers between devices, from_root(): return lax.psum(jnp.where(mine, value, jnp.zeros_like(value)), axis)  587 us
    ppermute x4, starting transfers between devices, passed_along(): lax.ppermute(value, axis, [(source, source + steps) for source in range(l...  16.8 us
    another operation x4, other arithmetic, body(): return (surface, jnp.stack(results)[None])  16.2 us
  transfers between devices with their start and end apart: 9, of which 2 were waited for; matrix products, arithmetic and copies ran while one was open for 7% of the time, Pallas kernels for 0%

commit v1 on v0

v1 whole, which is shorter than its diff:
```python
import functools

import jax
import jax.numpy as jnp
import numpy as np
from jax import lax
from jax.experimental import pallas as pl
from jax.experimental.pallas import tpu as pltpu
from jax.sharding import PartitionSpec as P

BLK = 64
LAGS = 32
SPAN = 4
NY = 4
TILES = 8
ROWS = 64
LANES = 128
MESH = pl.DeviceIdType.MESH
F32 = jnp.float32
BF16 = jnp.bfloat16

RIGHT, LEFT, VRIGHT, VLEFT, COLS, LINES, TABLE_ROWS = 0, 128, 256, 512, 544, 1056, 1248


def tables():
    n = np.arange(BLK)
    angle = 2.0 * np.pi / BLK * (n[:, None] * n[None, :] % BLK)
    cosine, sine = np.cos(angle), np.sin(angle)
    signed = np.where(n < BLK // 2, n, n - BLK)
    lag = np.arange(LAGS) - LAGS // 2
    lag_angle = 2.0 * np.pi / (2 * BLK) * (lag[:, None] * signed[None, :] % (2 * BLK))
    lag_cos, lag_sin = np.cos(lag_angle), np.sin(lag_angle)
    table = np.zeros((TABLE_ROWS, 256), np.float64)
    for b in range(2):
        rows = slice(RIGHT + 64 * b, RIGHT + 64 * b + 64)
        table[rows, 64 * b : 64 * b + 64] = cosine
        table[rows, 128 + 64 * b : 128 + 64 * b + 64] = sine
        top = VRIGHT + 128 * b
        table[top + 64 * b : top + 64 * b + 64, 0:128] = np.tile(lag_cos.T, (1, 4))
        table[top + 64 * b : top + 64 * b + 64, 128:256] = np.tile(lag_sin.T, (1, 4))
    table[LEFT : LEFT + 64, 0:64] = cosine
    table[LEFT : LEFT + 64, 64:128] = -sine
    table[LEFT + 64 : LEFT + 128, 0:64] = -sine
    table[LEFT + 64 : LEFT + 128, 64:128] = -cosine
    order = np.array([4 * q + i for i in range(4) for q in range(8)])
    table[VLEFT : VLEFT + 32] = np.concatenate([lag_cos, -lag_sin, -lag_sin, -lag_cos], axis=1)[order]
    c, r = np.arange(512)[:, None], np.arange(256)[None, :]
    table[COLS : COLS + 512] = np.abs(c - 128 - r) <= 9
    c, r = np.arange(192)[:, None], np.arange(192)[None, :]
    table[LINES : LINES + 192, 0:192] = (np.abs(c - r) <= 2) & (c // 64 == r // 64)
    return jnp.asarray(table, BF16)


def tap_rows(off_s, frac_s):
    row = lax.broadcasted_iota(jnp.int32, (16, LANES), 0)
    lane = lax.broadcasted_iota(jnp.int32, (16, LANES), 1)
    off = jnp.zeros((16, LANES), jnp.int32)
    frac = jnp.zeros((16, LANES), F32)
    for j in range(16):
        off = jnp.where(row == j, off_s[0, 0, j], off)
        frac = jnp.where(row == j, frac_s[0, 0, j], frac)
    u = jnp.where(lane < 64, -lane, 128 - lane) - off
    valid = (u >= -3) & (u <= 4)
    uf = u.astype(F32)
    x = uf - frac
    near = jnp.minimum(frac, 1.0 - frac)
    a = near * np.float32(np.pi)
    a2 = a * a
    series = np.float32(1.6059044e-10)
    for coefficient in (-2.5052108e-8, 2.7557319e-6, -1.9841270e-4, 8.3333333e-3, -1.6666667e-1, 1.0):
        series = series * a2 + np.float32(coefficient)
    sine = a * series
    sign = jnp.where((u & 1) == 0, -1.0, 1.0)
    zero = x == 0.0
    sinc = jnp.where(zero, 1.0, sign * sine / jnp.where(zero, 1.0, np.float32(np.pi) * x))
    b = x * np.float32(np.pi / 8)
    b2 = b * b
    half = np.float32(-1.1470746e-11)
    for coefficient in (2.0876757e-9, -2.7557319e-7, 2.4801587e-5, -1.3888889e-3, 4.1666667e-2, -0.5, 1.0):
        half = half * b2 + np.float32(coefficient)
    return jnp.where(valid, sinc * half * half, 0.0)


def resample_tile(s, samples, first, second, lane, diff):
    first = jnp.broadcast_to(first, (LANES, LANES))
    second = jnp.broadcast_to(second, (LANES, LANES))
    first = pltpu.roll(first, 0, 1, stride=1, stride_axis=0)
    second = pltpu.roll(second, 0, 1, stride=1, stride_axis=0)
    band = jnp.where(lane < 64, first, second)
    high = band.astype(BF16).astype(F32)
    low = band - high
    parts = []
    for keep in (diff >= 64, jnp.abs(diff) < 64, diff <= -64):
        parts.append(
            jnp.concatenate(
                [jnp.where(keep, high, 0.0).astype(BF16), jnp.where(keep, low, 0.0).astype(BF16)], axis=1
            )
        )
    weights = jnp.concatenate(parts, axis=0)
    window = jnp.concatenate(
        [samples[i].reshape(128, LANES) for i in ((s + 8) % 9, s, (s + 1) % 9)], axis=1
    )
    both = jnp.dot(window, weights, preferred_element_type=F32)
    return both[:, 0:LANES] + both[:, LANES:256]


def halves(rows, lane):
    left = jnp.sum(jnp.where(lane < 64, rows, 0.0), axis=1, keepdims=True)
    right = jnp.sum(jnp.where(lane < 64, 0.0, rows), axis=1, keepdims=True)
    return jnp.where(lane < 64, left, right)


def spectrum(amp, table, lane8):
    blocks = [amp[p].astype(F32) for p in range(TILES)]
    sums = jnp.concatenate([jnp.sum(b, axis=0, keepdims=True) for b in blocks], axis=0)
    mean = halves(sums, lane8) * np.float32(1.0 / (BLK * BLK))
    centered = [b - mean[p : p + 1] for p, b in enumerate(blocks)]
    squares = jnp.concatenate([jnp.sum(c * c, axis=0, keepdims=True) for c in centered], axis=0)
    energy = halves(squares, lane8)
    stacked = jnp.concatenate([c.astype(BF16) for c in centered], axis=0)
    along = jnp.dot(stacked, table[RIGHT : RIGHT + 128, :], preferred_element_type=F32)
    left = table[LEFT : LEFT + 128, 0:128]
    out = []
    for p in range(TILES):
        part = along[64 * p : 64 * p + 64]
        part = jnp.concatenate([part[:, 0:128], part[:, 128:256]], axis=0).astype(BF16)
        out.append(jnp.dot(left, part, preferred_element_type=F32))
    return out, energy


def surfaces(own_spec, own_energy, ref_parts, ref_energy, table, out, lane8):
    scale = 1.0 / (np.float32(BLK) * jnp.sqrt(own_energy * ref_energy + 1e-06))
    vleft = table[VLEFT : VLEFT + 32, :]
    for p in range(TILES):
        own_real, own_imag = own_spec[p, 0:64], own_spec[p, 64:128]
        ref_real, ref_imag = ref_parts[p][0:64], ref_parts[p][64:128]
        cross = jnp.concatenate(
            [own_real * ref_real + own_imag * ref_imag, own_imag * ref_real - own_real * ref_imag], axis=0
        ).astype(BF16)
        for b in range(2):
            right = table[VRIGHT + 128 * b : VRIGHT + 128 * b + 128, :]
            turned = jnp.dot(cross, right, preferred_element_type=F32)
            turned = jnp.concatenate([turned[:, 0:128], turned[:, 128:256]], axis=0).astype(BF16)
            value = jnp.dot(vleft, turned, preferred_element_type=F32)
            picked = value[0:8]
            for i in range(1, 4):
                picked = jnp.where(lane8 >= 32 * i, value[8 * i : 8 * i + 8], picked)
            picked = picked * jnp.broadcast_to(scale[p : p + 1, 64 * b : 64 * b + 1], (8, LANES))
            out[2 * p + b] = picked


def box_group(g, fields, rows, table, lines):
    window = jnp.concatenate(
        [fields[i, 0:rows] for i in ((2 * g + 8) % 9, 2 * g, 2 * g + 1, 2 * g + 2)], axis=1
    )
    summed = jnp.dot(window, table[COLS : COLS + 512, :], preferred_element_type=F32)
    return jnp.dot(lines, summed.astype(BF16), preferred_element_type=F32)


def kernel(
    nz, nx, nr,
    ref_s, off_s, frac_s, part_s, slc_h, table_h,
    surf_h, coh_h,
    table, samples, halo, taps, tap_halo, amp, masked, scatter, merged, exchange, ref_amp,
    own_spec, own, partner, fields, box_own, coh, surf,
    in_sem, halo_send, halo_recv, rs_send, rs_recv, ae_send, ae_recv, ag_send, ag_recv,
    own_send, relay_send, item_recv, out_sem,
):
    date, rng = lax.axis_index("date"), lax.axis_index("rng")
    planes = nx * nz
    nxy = nx * NY
    ts = TILES // nz
    plane, y = date // NY, date % NY
    z, xy = plane % nz, (plane // nz) * NY + y
    has_left, has_right = rng > 0, rng < nr - 1
    has_before, has_after = plane > 0, plane < planes - 1

    def z_date(k):
        return ((plane // nz) * nz + (z + k) % nz) * NY + y

    def xy_date(k):
        other = (xy + k) % nxy
        return ((other // NY) * nz + z) * NY + other % NY

    def remote(src, dst, send, recv, to_date, to_rng):
        return pltpu.make_async_remote_copy(
            src_ref=src, dst_ref=dst, send_sem=send, recv_sem=recv,
            device_id=(to_date, to_rng), device_id_type=MESH,
        )

    loads = [
        pltpu.make_async_copy(slc_h.at[0, :, :, pl.ds(128 * p, 128)], samples.at[p], in_sem.at[p])
        for p in range(TILES)
    ]
    for load in loads:
        load.start()
    table_load = pltpu.make_async_copy(table_h, table, in_sem.at[TILES])
    table_load.start()

    barrier = pltpu.get_barrier_semaphore()

    def hello(to_date, to_rng):
        pl.semaphore_signal(barrier, inc=1, device_id=(to_date, to_rng), device_id_type=MESH)

    for k in range(1, nz):
        hello(z_date(k), rng)
    for k in range(1, nxy):
        hello(xy_date(k), rng)
    for present, to_date, to_rng in (
        (has_left, date, rng - 1), (has_right, date, rng + 1),
        (has_before, date - NY, rng), (has_after, date + NY, rng),
    ):
        @pl.when(present)
        def _(to_date=to_date, to_rng=to_rng):
            hello(to_date, to_rng)

    lane = lax.broadcasted_iota(jnp.int32, (LANES, LANES), 1)
    diff = lax.broadcasted_iota(jnp.int32, (LANES, LANES), 0) - lane
    lane8 = lane[0:8]
    rows = tap_rows(off_s, frac_s)
    taps[...] = rows

    @pl.when(jnp.logical_not(has_left))
    def _():
        halo[0] = jnp.zeros((2, ROWS, LANES), BF16)
        tap_halo[0] = jnp.zeros((8, LANES), F32)

    @pl.when(jnp.logical_not(has_right))
    def _():
        halo[1] = jnp.zeros((2, ROWS, LANES), BF16)
        tap_halo[1] = jnp.zeros((8, LANES), F32)

    for h in range(1, SPAN + 1):
        @pl.when(jnp.logical_not(jnp.logical_or(y + h < NY, has_after)))
        def _(h=h):
            partner[h - 1] = jnp.zeros((9, 2, ROWS, LANES), BF16)

    root = jnp.where(ref_s[0] == date, 1.0, 0.0).astype(F32)
    for p in range(TILES):
        loads[p].wait()
        real, imag = samples[p, 0].astype(F32), samples[p, 1].astype(F32)
        size = jnp.sqrt(real * real + imag * imag + 1e-06).astype(BF16)
        amp[p] = size
        masked[p] = (size.astype(F32) * root).astype(BF16)

    greeted = (nz - 1) + (nxy - 1)
    for present in (has_left, has_right, has_before, has_after):
        greeted = greeted + present.astype(jnp.int32)
    pl.semaphore_wait(barrier, greeted)

    scatters = []
    for k in range(1, nz):
        to = (z + k) % nz
        scatters.append(
            remote(masked.at[pl.ds(to * ts, ts)], scatter.at[k - 1], rs_send.at[k - 1], rs_recv.at[k - 1],
                   z_date(k), rng)
        )
    to_left = [
        remote(samples.at[0], halo.at[1], halo_send.at[0], halo_recv.at[0], date, rng - 1),
        remote(taps.at[pl.ds(0, 8)], tap_halo.at[1], halo_send.at[1], halo_recv.at[1], date, rng - 1),
    ]
    to_right = [
        remote(samples.at[7], halo.at[0], halo_send.at[2], halo_recv.at[2], date, rng + 1),
        remote(taps.at[pl.ds(8, 8)], tap_halo.at[0], halo_send.at[3], halo_recv.at[3], date, rng + 1),
    ]

    @pl.when(has_left)
    def _():
        for copy in to_left:
            copy.start()

    @pl.when(has_right)
    def _():
        for copy in to_right:
            copy.start()

    for copy in scatters:
        copy.start()

    chunks = ((1, 6), (7, 2), (0, 1))
    nc = len(chunks)

    def item_copies(source, c, slot, send, to_date):
        start, count = chunks[c]
        return remote(
            source.at[pl.ds(start, count)], partner.at[slot, pl.ds(start, count)],
            send, item_recv.at[slot, c], to_date, rng,
        )

    own_dests = [(has_before, SPAN - 1, date - NY)] + [(y >= k, k - 1, date - k) for k in range(1, NY)]
    own_copies = [
        [item_copies(own, c, slot, own_send.at[i, c], to) for c in range(nc)]
        for i, (_, slot, to) in enumerate(own_dests)
    ]
    relay_dests = [
        (jnp.logical_and(has_after, y + k < NY), SPAN - k - 1, date + k) for k in range(1, NY)
    ]
    relay_copies = [
        [item_copies(partner.at[SPAN - 1], c, slot, relay_send.at[i, c], to) for c in range(nc)]
        for i, (_, slot, to) in enumerate(relay_dests)
    ]

    def send_own(c):
        for (present, _, _), copies in zip(own_dests, own_copies):
            @pl.when(present)
            def _(copies=copies):
                copies[c].start()

    def store_own(s, keep=None):
        if s < TILES:
            first, second = rows[2 * s : 2 * s + 1], rows[2 * s + 1 : 2 * s + 2]
        else:
            first, second = tap_halo[1][0:1], tap_halo[0][7:8]
        tile = resample_tile(s, samples, first, second, lane, diff)
        if keep is not None:
            tile = jnp.where(keep, tile, 0.0)
        own[s] = tile.astype(BF16).reshape(2, ROWS, LANES)

    for s in range(1, 7):
        store_own(s)
    send_own(0)

    @pl.when(has_right)
    def _():
        to_left[0].wait_recv()
        to_left[1].wait_recv()

    @pl.when(has_left)
    def _():
        to_right[0].wait_recv()
        to_right[1].wait_recv()

    lane_h = lax.broadcasted_iota(jnp.int32, (2, ROWS, LANES), 2)
    samples[8] = jnp.where(lane_h < 64, halo[1].astype(F32), halo[0].astype(F32)).astype(BF16)
    low_edge = jnp.where(has_right, 64, 0)
    high_edge = jnp.where(has_left, 64, 128)
    store_own(7)
    store_own(8, jnp.logical_or(lane < low_edge, lane >= high_edge))
    send_own(1)
    store_own(0)
    send_own(2)

    table_load.wait()
    parts, own_energy = spectrum(amp, table, lane8)
    for p in range(TILES):
        own_spec[p] = parts[p]

    for copy in scatters:
        copy.wait_recv()
    total = masked[pl.ds(z * ts, ts)].astype(F32)
    for k in range(nz - 1):
        total = total + scatter[k].astype(F32)
    merged[...] = total.astype(BF16)
    exchanges = [
        remote(merged, exchange.at[k - 1], ae_send.at[k - 1], ae_recv.at[k - 1], xy_date(k), rng)
        for k in range(1, nxy)
    ]
    for copy in exchanges:
        copy.start()

    lines = table[LINES : LINES + 192, 0:192]
    for s in range(9):
        real, imag = own[s, 0].astype(F32), own[s, 1].astype(F32)
        fields[s, 0:64] = (real * real + imag * imag).astype(BF16)
    for g in range(4):
        box_own[:, 256 * g : 256 * g + 256] = box_group(g, fields, 64, table, table[LINES : LINES + 64, 0:64])

    for c in range(nc):
        @pl.when(has_after)
        def _(c=c):
            own_copies[0][c].wait_recv()

        for (present, _, _), copies in zip(relay_dests, relay_copies):
            @pl.when(present)
            def _(copies=copies):
                copies[c].start()

    outs = []

    def pair(h):
        slot = h - 1
        if h < SPAN:
            @pl.when(jnp.logical_or(y + h < NY, has_after))
            def _():
                for c in range(nc):
                    own_copies[h][c].wait_recv()
        for s in range(9):
            own0, own1 = own[s, 0].astype(F32), own[s, 1].astype(F32)
            other0, other1 = partner[slot, s, 0].astype(F32), partner[slot, s, 1].astype(F32)
            fields[s, 0:64] = (own0 * other0 + own1 * other1).astype(BF16)
            fields[s, 64:128] = (own1 * other0 - own0 * other1).astype(BF16)
            fields[s, 128:192] = (other0 * other0 + other1 * other1).astype(BF16)
        weight = part_s[0, slot].astype(F32)
        for g in range(4):
            box = box_group(g, fields, 192, table, lines)
            re, im, power = box[0:64], box[64:128], box[128:192]
            mine = box_own[:, 256 * g : 256 * g + 256]
            value = weight * (re * re + im * im) / (mine * power + 1e-06)
            coh[slot, :, 256 * g : 256 * g + 256] = value.astype(BF16)
        out = pltpu.make_async_copy(coh.at[slot], coh_h.at[0, slot], out_sem.at[slot])
        out.start()
        outs.append(out)

    pair(4)

    for copy in exchanges:
        copy.wait_recv()
    total = merged[...].astype(F32)
    for k in range(nxy - 1):
        total = total + exchange[k].astype(F32)
    ref_amp[pl.ds(z * ts, ts)] = total.astype(BF16)
    mine = ref_amp.at[pl.ds(z * ts, ts)]
    gathers = [
        remote(mine, mine, ag_send.at[k - 1], ag_recv.at[k - 1], z_date(k), rng) for k in range(1, nz)
    ]
    for copy in gathers:
        copy.start()

    pair(1)
    pair(2)

    for copy in gathers:
        copy.wait_recv()
    ref_parts, ref_energy = spectrum(ref_amp, table, lane8)
    surfaces(own_spec, own_energy, ref_parts, ref_energy, table, surf, lane8)
    out = pltpu.make_async_copy(surf, surf_h.at[0, 0], out_sem.at[SPAN])
    out.start()
    outs.append(out)

    pair(3)

    for copy in scatters + exchanges + gathers:
        copy.wait_send()

    @pl.when(has_left)
    def _():
        for copy in to_left:
            copy.wait_send()

    @pl.when(has_right)
    def _():
        for copy in to_right:
            copy.wait_send()

    for dests, copies in ((own_dests, own_copies), (relay_dests, relay_copies)):
        for (present, _, _), mine in zip(dests, copies):
            @pl.when(present)
            def _(mine=mine):
                for copy in mine:
                    copy.wait_send()
    for out in outs:
        out.wait()


def body(nz, nx, nr, slc, ref_date, int_offset, frac_offset, partners):
    ts = TILES // nz
    nxy = nx * NY
    smem = pl.BlockSpec(memory_space=pltpu.SMEM)
    anywhere = pl.BlockSpec(memory_space=pl.ANY)
    dma = pltpu.SemaphoreType.DMA
    tile = (2, ROWS, LANES)
    slab = (TILES, ROWS, LANES)
    surface, coherence = pl.pallas_call(
        functools.partial(kernel, nz, nx, nr),
        out_shape=(
            jax.ShapeDtypeStruct((1, 1, 16, 8, LANES), F32),
            jax.ShapeDtypeStruct((1, SPAN, ROWS, TILES * LANES), BF16),
        ),
        in_specs=[smem, smem, smem, smem, anywhere, anywhere],
        out_specs=(anywhere, anywhere),
        scratch_shapes=[
            pltpu.VMEM((TABLE_ROWS, 256), BF16),
            pltpu.VMEM((9,) + tile, BF16),
            pltpu.VMEM((2,) + tile, BF16),
            pltpu.VMEM((16, LANES), F32),
            pltpu.VMEM((2, 8, LANES), F32),
            pltpu.VMEM(slab, BF16),
            pltpu.VMEM(slab, BF16),
            pltpu.VMEM((max(nz - 1, 1), ts, ROWS, LANES), BF16),
            pltpu.VMEM((ts, ROWS, LANES), BF16),
            pltpu.VMEM((nxy - 1, ts, ROWS, LANES), BF16),
            pltpu.VMEM(slab, BF16),
            pltpu.VMEM((TILES, 128, LANES), F32),
            pltpu.VMEM((9,) + tile, BF16),
            pltpu.VMEM((SPAN, 9) + tile, BF16),
            pltpu.VMEM((9, 192, LANES), BF16),
            pltpu.VMEM((ROWS, TILES * LANES), F32),
            pltpu.VMEM((SPAN, ROWS, TILES * LANES), BF16),
            pltpu.VMEM((16, 8, LANES), F32),
            dma((TILES + 1,)),
            dma((4,)), dma((4,)),
            dma((max(nz - 1, 1),)), dma((max(nz - 1, 1),)),
            dma((nxy - 1,)), dma((nxy - 1,)),
            dma((max(nz - 1, 1),)), dma((max(nz - 1, 1),)),
            dma((4, 3)), dma((3, 3)), dma((4, 3)),
            dma((SPAN + 1,)),
        ],
        compiler_params=pltpu.CompilerParams(collective_id=0, has_side_effects=True),
    )(ref_date, int_offset, frac_offset, partners, slc, tables())
    return surface.reshape(1, 1, 16, 1024), coherence


def solution(mesh):
    dates, nr = mesh.shape["date"], mesh.shape["rng"]
    planes = dates // NY
    nz = min(planes, 8)
    in_specs = (
        P("date", None, None, "rng"),
        P(),
        P("date", None, "rng"),
        P("date", None, "rng"),
        P("date", None),
    )
    out_specs = (P("date", None, "rng", None), P("date", None, None, "rng"))
    return jax.shard_map(
        functools.partial(body, nz, planes // nz, nr),
        mesh=mesh, in_specs=in_specs, out_specs=out_specs, check_vma=False,
    )
```

time: 715 us -> 44.3 us (0.06); the launches traced: 702 us -> 44.1 us
  waiting for transfers between devices: 588 us -> 0 us
  Pallas kernels: 0 us -> 39.5 us
  other arithmetic: 30.7 us -> 0 us
  starting transfers between devices: 25.4 us -> 0 us
  local copies, waits for them, and re-layouts: 25.3 us -> 3.35 us
  between operations: 18.1 us -> 1.28 us
  matrix products: 14.2 us -> 0 us
    psum x1 -> x0, waiting for transfers between devices: 587 us -> none  [from_root(): return lax.psum(jnp.where(mine, value, jnp.zeros_like(value)), axis)]
    pallas_call x0 -> x1, Pallas kernels: none -> 39.5 us  [body(): pl.pallas_call(functools.partial(kernel, nz, nx, nr), out_shape=(jax.Shap...]
    ppermute x8 -> x0, starting transfers between devices: 25.4 us -> none  [the longest x4 16.8 us: passed_along(): lax.ppermute(value, axis, [(source, source + steps) for source in range(l...]
    another operation x4 -> x0, other arithmetic: 16.2 us -> none  [body(): return (surface, jnp.stack(results)[None])]
    dot_general x18 -> x0, matrix products: 14.2 us -> none  [the longest x2 2.04 us: spectra(): jnp.einsum('abkn,ln->abkl', first_imag, cosine, precision=HIGHEST)]
    unnamed x24 -> x1, local copies, waits for them, and re-layouts: 13.9 us -> 1.87 us
  transfers between devices with their start and end apart: 9 -> 0, of which waited for: 2 -> 0; matrix products, arithmetic and copies ran while one was open for 7% -> 0% of each run, Pallas kernels for 0% -> 0%
where the time goes in v1:
time: 44.3 us; the launch traced here: 44.1 us
  Pallas kernels  39.5 us (89%)
  local copies, waits for them, and re-layouts  3.35 us (8%)
  between operations  1.28 us (3%)
    pallas_call x1, Pallas kernels, body(): pl.pallas_call(functools.partial(kernel, nz, nx, nr), out_shape=(jax.Shap...  39.5 us
    unnamed x1, local copies, waits for them, and re-layouts  1.87 us
    reshape x1, local copies, waits for them, and re-layouts, body(): return (surface.reshape(1, 1, 16, 1024), coherence)  1.49 us

profile of v1, /device:TPU:24, one launch (start us, length us, event | category | flops | bytes accessed | tf_op | source)
XLA Modules:
  0.0 44.1 jit_solution(9515345140842231322)
XLA Ops:
  1.3 39.5 %shard_map.77 = (f32[1,1,16,8,128]{4,3,2,1,0:T(8,128)}, bf16[1,4,64,1024]{3,2,1,0:T(8,128)(2,1)}) custom-call(s32[1]{0:T(128)S(6)} %copy.9.ref_s, s32[1,1,16]{2,1,0:T(1,128)} %off_s.1, f32[1,1,16]{2,1,0:T(1,128)} %frac_s.1, s32[1,4]{1,0:T(1,128)} %part_s.1, bf16[1,2,64,1024]{3,2,1,0:T(8,128)(2,1)} %slc_h.1, bf16[1248,256]{1,0:T(8,128)(2,1)} %constant.2.clone.table_h), custom_call_target="tpu_custom_call" | custom-call | tf_op jit(solution)/shard_map/pallas_call | solution.py:463
  40.7 1.5 %reshape.7 = f32[1,1,16,1024]{3,2,1,0:T(8,128)} reshape(f32[1,1,16,8,128]{4,3,2,1,0:T(8,128)} %get-tuple-element.4) | data formatting | bytes 131072 | tf_op jit(solution)/shard_map/reshape | solution.py:500
  42.2 1.9 %copy.10 = bf16[1,4,64,1024]{3,2,1,0:T(8,128)(2,1)} copy(bf16[1,4,64,1024]{3,2,1,0:T(8,128)(2,1)} %get-tuple-element.9) | data formatting | bytes 1048576

commit v2 on v1

--- a/solution.py
+++ b/solution.py
@@ -35,9 +35,10 @@
         rows = slice(RIGHT + 64 * b, RIGHT + 64 * b + 64)
         table[rows, 64 * b : 64 * b + 64] = cosine
         table[rows, 128 + 64 * b : 128 + 64 * b + 64] = sine
-        top = VRIGHT + 128 * b
-        table[top + 64 * b : top + 64 * b + 64, 0:128] = np.tile(lag_cos.T, (1, 4))
-        table[top + 64 * b : top + 64 * b + 64, 128:256] = np.tile(lag_sin.T, (1, 4))
+        rows = slice(VRIGHT + 64 * b, VRIGHT + 64 * b + 64)
+        table[rows, 128 * b : 128 * b + 128] = np.tile(lag_cos.T, (1, 4))
+        rows = slice(VRIGHT + 128 + 64 * b, VRIGHT + 128 + 64 * b + 64)
+        table[rows, 128 * b : 128 * b + 128] = np.tile(lag_sin.T, (1, 4))
     table[LEFT : LEFT + 64, 0:64] = cosine
     table[LEFT : LEFT + 64, 64:128] = -sine
     table[LEFT + 64 : LEFT + 128, 0:64] = -sine
@@ -137,16 +138,17 @@
         cross = jnp.concatenate(
             [own_real * ref_real + own_imag * ref_imag, own_imag * ref_real - own_real * ref_imag], axis=0
         ).astype(BF16)
+        turned = [
+            jnp.dot(cross, table[top : top + 128, :], preferred_element_type=F32).astype(BF16)
+            for top in (VRIGHT, VRIGHT + 128)
+        ]
+        value = jnp.dot(vleft, jnp.concatenate(turned, axis=0), preferred_element_type=F32)
         for b in range(2):
-            right = table[VRIGHT + 128 * b : VRIGHT + 128 * b + 128, :]
-            turned = jnp.dot(cross, right, preferred_element_type=F32)
-            turned = jnp.concatenate([turned[:, 0:128], turned[:, 128:256]], axis=0).astype(BF16)
-            value = jnp.dot(vleft, turned, preferred_element_type=F32)
-            picked = value[0:8]
+            half = value[:, 128 * b : 128 * b + 128]
+            picked = half[0:8]
             for i in range(1, 4):
-                picked = jnp.where(lane8 >= 32 * i, value[8 * i : 8 * i + 8], picked)
-            picked = picked * jnp.broadcast_to(scale[p : p + 1, 64 * b : 64 * b + 1], (8, LANES))
-            out[2 * p + b] = picked
+                picked = jnp.where(lane8 >= 32 * i, half[8 * i : 8 * i + 8], picked)
+            out[2 * p + b] = picked * jnp.broadcast_to(scale[p : p + 1, 64 * b : 64 * b + 1], (8, LANES))
 
 
 def box_group(g, fields, rows, table, lines):
@@ -160,11 +162,11 @@
 def kernel(
     nz, nx, nr,
     ref_s, off_s, frac_s, part_s, slc_h, table_h,
-    surf_h, coh_h,
+    surf, coh,
     table, samples, halo, taps, tap_halo, amp, masked, scatter, merged, exchange, ref_amp,
-    own_spec, own, partner, fields, box_own, coh, surf,
+    own_spec, own, partner, fields, box_own,
     in_sem, halo_send, halo_recv, rs_send, rs_recv, ae_send, ae_recv, ag_send, ag_recv,
-    own_send, relay_send, item_recv, out_sem,
+    own_send, relay_send, item_recv,
 ):
     date, rng = lax.axis_index("date"), lax.axis_index("rng")
     planes = nx * nz
@@ -233,7 +235,7 @@
     for h in range(1, SPAN + 1):
         @pl.when(jnp.logical_not(jnp.logical_or(y + h < NY, has_after)))
         def _(h=h):
-            partner[h - 1] = jnp.zeros((9, 2, ROWS, LANES), BF16)
+            coh[h - 1] = jnp.zeros((ROWS, TILES * LANES), BF16)
 
     root = jnp.where(ref_s[0] == date, 1.0, 0.0).astype(F32)
     for p in range(TILES):
@@ -340,11 +342,6 @@
     store_own(0)
     send_own(2)
 
-    table_load.wait()
-    parts, own_energy = spectrum(amp, table, lane8)
-    for p in range(TILES):
-        own_spec[p] = parts[p]
-
     for copy in scatters:
         copy.wait_recv()
     total = masked[pl.ds(z * ts, ts)].astype(F32)
@@ -358,16 +355,14 @@
     for copy in exchanges:
         copy.start()
 
-    lines = table[LINES : LINES + 192, 0:192]
-    for s in range(9):
-        real, imag = own[s, 0].astype(F32), own[s, 1].astype(F32)
-        fields[s, 0:64] = (real * real + imag * imag).astype(BF16)
-    for g in range(4):
-        box_own[:, 256 * g : 256 * g + 256] = box_group(g, fields, 64, table, table[LINES : LINES + 64, 0:64])
-
-    for c in range(nc):
+    table_load.wait()
+    parts, own_energy = spectrum(amp, table, lane8)
+    for p in range(TILES):
+        own_spec[p] = parts[p]
+
+    def relay(c):
         @pl.when(has_after)
-        def _(c=c):
+        def _():
             own_copies[0][c].wait_recv()
 
         for (present, _, _), copies in zip(relay_dests, relay_copies):
@@ -375,15 +370,36 @@
             def _(copies=copies):
                 copies[c].start()
 
-    outs = []
+    relay(0)
+
+    for s in range(9):
+        real, imag = own[s, 0].astype(F32), own[s, 1].astype(F32)
+        fields[s, 0:64] = (real * real + imag * imag).astype(BF16)
+    lines = table[LINES : LINES + 192, 0:192]
+    for g in range(4):
+        box_own[:, 256 * g : 256 * g + 256] = box_group(g, fields, 64, table, table[LINES : LINES + 64, 0:64])
+
+    for copy in exchanges:
+        copy.wait_recv()
+    total = merged[...].astype(F32)
+    for k in range(nxy - 1):
+        total = total + exchange[k].astype(F32)
+    ref_amp[pl.ds(z * ts, ts)] = total.astype(BF16)
+    mine = ref_amp.at[pl.ds(z * ts, ts)]
+    gathers = [
+        remote(mine, mine, ag_send.at[k - 1], ag_recv.at[k - 1], z_date(k), rng) for k in range(1, nz)
+    ]
+    for copy in gathers:
+        copy.start()
+
+    relay(1)
+    relay(2)
 
     def pair(h):
         slot = h - 1
         if h < SPAN:
-            @pl.when(jnp.logical_or(y + h < NY, has_after))
-            def _():
-                for c in range(nc):
-                    own_copies[h][c].wait_recv()
+            for c in range(nc):
+                own_copies[h][c].wait_recv()
         for s in range(9):
             own0, own1 = own[s, 0].astype(F32), own[s, 1].astype(F32)
             other0, other1 = partner[slot, s, 0].astype(F32), partner[slot, s, 1].astype(F32)
@@ -397,37 +413,27 @@
             mine = box_own[:, 256 * g : 256 * g + 256]
             value = weight * (re * re + im * im) / (mine * power + 1e-06)
             coh[slot, :, 256 * g : 256 * g + 256] = value.astype(BF16)
-        out = pltpu.make_async_copy(coh.at[slot], coh_h.at[0, slot], out_sem.at[slot])
-        out.start()
-        outs.append(out)
-
-    pair(4)
-
-    for copy in exchanges:
-        copy.wait_recv()
-    total = merged[...].astype(F32)
-    for k in range(nxy - 1):
-        total = total + exchange[k].astype(F32)
-    ref_amp[pl.ds(z * ts, ts)] = total.astype(BF16)
-    mine = ref_amp.at[pl.ds(z * ts, ts)]
-    gathers = [
-        remote(mine, mine, ag_send.at[k - 1], ag_recv.at[k - 1], z_date(k), rng) for k in range(1, nz)
-    ]
-    for copy in gathers:
-        copy.start()
-
-    pair(1)
-    pair(2)
+
+    @pl.when(has_after)
+    def _():
+        pair(SPAN)
+
+    for h in range(1, NY):
+        @pl.when(y + h < NY)
+        def _(h=h):
+            pair(h)
 
     for copy in gathers:
         copy.wait_recv()
     ref_parts, ref_energy = spectrum(ref_amp, table, lane8)
     surfaces(own_spec, own_energy, ref_parts, ref_energy, table, surf, lane8)
-    out = pltpu.make_async_copy(surf, surf_h.at[0, 0], out_sem.at[SPAN])
-    out.start()
-    outs.append(out)
-
-    pair(3)
+
+    for h in range(1, NY):
+        @pl.when(y + h >= NY)
+        def _(h=h):
+            @pl.when(has_after)
+            def _():
+                pair(h)
 
     for copy in scatters + exchanges + gathers:
         copy.wait_send()
@@ -448,8 +454,17 @@
             def _(mine=mine):
                 for copy in mine:
                     copy.wait_send()
-    for out in outs:
-        out.wait()
+
+
+def write_kernel(surf, coh, surf_h, coh_h, rows, sem):
+    large = pltpu.make_async_copy(coh, coh_h.at[0], sem.at[0])
+    large.start()
+    for q in range(8):
+        rows[:, 128 * q : 128 * q + 128] = surf[:, q, :]
+    small = pltpu.make_async_copy(rows, surf_h.at[0, 0], sem.at[1])
+    small.start()
+    large.wait()
+    small.wait()
 
 
 def body(nz, nx, nr, slc, ref_date, int_offset, frac_offset, partners):
@@ -457,17 +472,18 @@
     nxy = nx * NY
     smem = pl.BlockSpec(memory_space=pltpu.SMEM)
     anywhere = pl.BlockSpec(memory_space=pl.ANY)
+    vmem = pl.BlockSpec(memory_space=pltpu.VMEM)
     dma = pltpu.SemaphoreType.DMA
     tile = (2, ROWS, LANES)
     slab = (TILES, ROWS, LANES)
     surface, coherence = pl.pallas_call(
         functools.partial(kernel, nz, nx, nr),
         out_shape=(
-            jax.ShapeDtypeStruct((1, 1, 16, 8, LANES), F32),
-            jax.ShapeDtypeStruct((1, SPAN, ROWS, TILES * LANES), BF16),
+            pltpu.VMEM((16, 8, LANES), F32),
+            pltpu.VMEM((SPAN, ROWS, TILES * LANES), BF16),
         ),
         in_specs=[smem, smem, smem, smem, anywhere, anywhere],
-        out_specs=(anywhere, anywhere),
+        out_specs=(vmem, vmem),
         scratch_shapes=[
             pltpu.VMEM((TABLE_ROWS, 256), BF16),
             pltpu.VMEM((9,) + tile, BF16),
@@ -485,19 +501,25 @@
             pltpu.VMEM((SPAN, 9) + tile, BF16),
             pltpu.VMEM((9, 192, LANES), BF16),
             pltpu.VMEM((ROWS, TILES * LANES), F32),
-            pltpu.VMEM((SPAN, ROWS, TILES * LANES), BF16),
-            pltpu.VMEM((16, 8, LANES), F32),
             dma((TILES + 1,)),
             dma((4,)), dma((4,)),
             dma((max(nz - 1, 1),)), dma((max(nz - 1, 1),)),
             dma((nxy - 1,)), dma((nxy - 1,)),
             dma((max(nz - 1, 1),)), dma((max(nz - 1, 1),)),
             dma((4, 3)), dma((3, 3)), dma((4, 3)),
-            dma((SPAN + 1,)),
         ],
         compiler_params=pltpu.CompilerParams(collective_id=0, has_side_effects=True),
     )(ref_date, int_offset, frac_offset, partners, slc, tables())
-    return surface.reshape(1, 1, 16, 1024), coherence
+    return pl.pallas_call(
+        write_kernel,
+        out_shape=(
+            jax.ShapeDtypeStruct((1, 1, 16, 1024), F32),
+            jax.ShapeDtypeStruct((1, SPAN, ROWS, TILES * LANES), BF16),
+        ),
+        in_specs=[vmem, vmem],
+        out_specs=(anywhere, anywhere),
+        scratch_shapes=[pltpu.VMEM((16, 1024), F32), dma((2,))],
+    )(*(pltpu.with_memory_space_constraint(x, pltpu.VMEM) for x in (surface, coherence)))
 
 
 def solution(mesh):

time: 44.3 us -> 38 us (0.86)
  the two profiles are of different devices: /device:TPU:24 before, /device:TPU:8 now
where the time goes in v2:
time: 38 us; the launch traced here: 37.9 us
  Pallas kernels  36.6 us (96%)
  between operations  1.28 us (3%)
    pallas_call x1, Pallas kernels, body(): pl.pallas_call(functools.partial(kernel, nz, nx, nr), out_shape=(pltpu.VM...  35.8 us
    pallas_call x1, Pallas kernels, body(): pl.pallas_call(write_kernel, out_shape=(jax.ShapeDtypeStruct((1, 1, 16, 1...  0.82 us

profile of v2, /device:TPU:8, one launch (start us, length us, event | category | flops | bytes accessed | tf_op | source)
XLA Modules:
  0.0 37.9 jit_solution(18084379497347601196)
XLA Ops:
  1.3 35.8 %shard_map.77 = (f32[16,8,128]{2,1,0:T(8,128)S(1)}, bf16[4,64,1024]{2,1,0:T(8,128)(2,1)S(1)}) custom-call(s32[1]{0:T(128)S(6)} %copy.8.ref_s, s32[1,1,16]{2,1,0:T(1,128)} %off_s.1, f32[1,1,16]{2,1,0:T(1,128)} %frac_s.1, s32[1,4]{1,0:T(1,128)} %part_s.1, bf16[1,2,64,1024]{3,2,1,0:T(8,128)(2,1)} %slc_h.1, bf16[1248,256]{1,0:T(8,128)(2,1)} %constant.2.clone.table_h), custom_call_target="tpu_custom_call" | custom-call | tf_op jit(solution)/shard_map/pallas_call | solution.py:479
  37.1 0.8 %shard_map.78 = (f32[1,1,16,1024]{3,2,1,0:T(8,128)}, bf16[1,4,64,1024]{3,2,1,0:T(8,128)(2,1)}) custom-call(f32[16,8,128]{2,1,0:T(8,128)S(1)} %get-tuple-element.4.surf, bf16[4,64,1024]{2,1,0:T(8,128)(2,1)S(1)} %get-tuple-element.5.coh), custom_call_target="tpu_custom_call" | custom-call | tf_op jit(solution)/shard_map/pallas_call | solution.py:513

commit v3 on v2

--- a/solution.py
+++ b/solution.py
@@ -120,29 +120,34 @@
     energy = halves(squares, lane8)
     stacked = jnp.concatenate([c.astype(BF16) for c in centered], axis=0)
     along = jnp.dot(stacked, table[RIGHT : RIGHT + 128, :], preferred_element_type=F32)
-    left = table[LEFT : LEFT + 128, 0:128]
-    out = []
+    parts = []
     for p in range(TILES):
         part = along[64 * p : 64 * p + 64]
-        part = jnp.concatenate([part[:, 0:128], part[:, 128:256]], axis=0).astype(BF16)
-        out.append(jnp.dot(left, part, preferred_element_type=F32))
-    return out, energy
+        parts.append(jnp.concatenate([part[:, 0:128], part[:, 128:256]], axis=0).astype(BF16))
+    full = jnp.dot(
+        table[LEFT : LEFT + 128, 0:128], jnp.concatenate(parts, axis=1), preferred_element_type=F32
+    )
+    return [full[:, 128 * p : 128 * p + 128] for p in range(TILES)], energy
 
 
 def surfaces(own_spec, own_energy, ref_parts, ref_energy, table, out, lane8):
     scale = 1.0 / (np.float32(BLK) * jnp.sqrt(own_energy * ref_energy + 1e-06))
     vleft = table[VLEFT : VLEFT + 32, :]
+    crosses = []
     for p in range(TILES):
         own_real, own_imag = own_spec[p, 0:64], own_spec[p, 64:128]
         ref_real, ref_imag = ref_parts[p][0:64], ref_parts[p][64:128]
-        cross = jnp.concatenate(
-            [own_real * ref_real + own_imag * ref_imag, own_imag * ref_real - own_real * ref_imag], axis=0
-        ).astype(BF16)
-        turned = [
-            jnp.dot(cross, table[top : top + 128, :], preferred_element_type=F32).astype(BF16)
-            for top in (VRIGHT, VRIGHT + 128)
-        ]
-        value = jnp.dot(vleft, jnp.concatenate(turned, axis=0), preferred_element_type=F32)
+        crosses.append((own_real * ref_real + own_imag * ref_imag).astype(BF16))
+        crosses.append((own_imag * ref_real - own_real * ref_imag).astype(BF16))
+    crosses = jnp.concatenate(crosses, axis=0)
+    cos_part, sin_part = (
+        jnp.dot(crosses, table[top : top + 128, :], preferred_element_type=F32).astype(BF16)
+        for top in (VRIGHT, VRIGHT + 128)
+    )
+    for p in range(TILES):
+        rows = slice(128 * p, 128 * p + 128)
+        turned = jnp.concatenate([cos_part[rows], sin_part[rows]], axis=0)
+        value = jnp.dot(vleft, turned, preferred_element_type=F32)
         for b in range(2):
             half = value[:, 128 * b : 128 * b + 128]
             picked = half[0:8]
@@ -151,12 +156,34 @@
             out[2 * p + b] = picked * jnp.broadcast_to(scale[p : p + 1, 64 * b : 64 * b + 1], (8, LANES))
 
 
-def box_group(g, fields, rows, table, lines):
-    window = jnp.concatenate(
-        [fields[i, 0:rows] for i in ((2 * g + 8) % 9, 2 * g, 2 * g + 1, 2 * g + 2)], axis=1
-    )
-    summed = jnp.dot(window, table[COLS : COLS + 512, :], preferred_element_type=F32)
-    return jnp.dot(lines, summed.astype(BF16), preferred_element_type=F32)
+def at(s):
+    return (s + 1) % TILES if s < TILES else TILES
+
+
+def pack_edge(tile, lane):
+    turned = pltpu.roll(tile, 16, 1)
+    packed = turned[0:32]
+    for k in range(1, 4):
+        packed = jnp.where(lane[0:32] >= 32 * k, pltpu.roll(turned[32 * k : 32 * k + 32], 32 * k, 1), packed)
+    return packed
+
+
+def unpack_edge(packed, lane):
+    keep = jnp.logical_or(lane[0:32] < 16, lane[0:32] >= 112)
+    parts = [jnp.where(keep, pltpu.roll(packed, 112 - 32 * k, 1), 0.0) for k in range(4)]
+    return jnp.concatenate(parts, axis=0)
+
+
+def boxes(fields, rows, table):
+    windows = [
+        jnp.concatenate([fields[i, 0:rows] for i in ((2 * g + 8) % 9, 2 * g, 2 * g + 1, 2 * g + 2)], axis=1)
+        for g in range(4)
+    ]
+    summed = jnp.dot(
+        jnp.concatenate(windows, axis=0), table[COLS : COLS + 512, :], preferred_element_type=F32
+    ).astype(BF16)
+    summed = jnp.concatenate([summed[rows * g : rows * g + rows] for g in range(4)], axis=1)
+    return jnp.dot(table[LINES : LINES + rows, 0:rows], summed, preferred_element_type=F32)
 
 
 def kernel(
@@ -164,7 +191,7 @@
     ref_s, off_s, frac_s, part_s, slc_h, table_h,
     surf, coh,
     table, samples, halo, taps, tap_halo, amp, masked, scatter, merged, exchange, ref_amp,
-    own_spec, own, partner, fields, box_own,
+    own_spec, own, edge, partner, partner_edge, fields, box_own,
     in_sem, halo_send, halo_recv, rs_send, rs_recv, ae_send, ae_recv, ag_send, ag_recv,
     own_send, relay_send, item_recv,
 ):
@@ -279,34 +306,48 @@
     for copy in scatters:
         copy.start()
 
-    chunks = ((1, 6), (7, 2), (0, 1))
-    nc = len(chunks)
-
-    def item_copies(source, c, slot, send, to_date):
-        start, count = chunks[c]
-        return remote(
-            source.at[pl.ds(start, count)], partner.at[slot, pl.ds(start, count)],
-            send, item_recv.at[slot, c], to_date, rng,
+    chunks = ((2, 6), (0, 2))
+    nc = len(chunks) + 1
+
+    def item_copies(source, source_edge, slot, sends, to_date):
+        copies = [
+            remote(
+                source.at[pl.ds(start, count)], partner.at[slot, pl.ds(start, count)],
+                sends.at[c], item_recv.at[slot, c], to_date, rng,
+            )
+            for c, (start, count) in enumerate(chunks)
+        ]
+        copies.append(
+            remote(source_edge, partner_edge.at[slot], sends.at[nc - 1], item_recv.at[slot, nc - 1], to_date, rng)
         )
-
-    own_dests = [(has_before, SPAN - 1, date - NY)] + [(y >= k, k - 1, date - k) for k in range(1, NY)]
-    own_copies = [
-        [item_copies(own, c, slot, own_send.at[i, c], to) for c in range(nc)]
-        for i, (_, slot, to) in enumerate(own_dests)
-    ]
+        return copies
+
+    own_dests = [(has_before, 3, date - NY), (y >= 1, 0, date - 1), (y >= 3, 2, date - 3)]
+    own_copies = [item_copies(own, edge, slot, own_send.at[i], to) for i, (_, slot, to) in enumerate(own_dests)]
+    middle = jnp.logical_and(y >= 1, y + 1 < NY)
     relay_dests = [
-        (jnp.logical_and(has_after, y + k < NY), SPAN - k - 1, date + k) for k in range(1, NY)
+        (jnp.logical_and(has_after, y + 1 < NY), 3, 2, date + 1),
+        (jnp.logical_and(has_after, y + 3 < NY), 3, 0, date + 3),
+        (middle, 0, 1, date - 1),
+        (jnp.logical_and(has_after, middle), 2, 1, date + 1),
     ]
     relay_copies = [
-        [item_copies(partner.at[SPAN - 1], c, slot, relay_send.at[i, c], to) for c in range(nc)]
-        for i, (_, slot, to) in enumerate(relay_dests)
-    ]
-
-    def send_own(c):
-        for (present, _, _), copies in zip(own_dests, own_copies):
-            @pl.when(present)
-            def _(copies=copies):
-                copies[c].start()
+        item_copies(partner.at[source], partner_edge.at[source], slot, relay_send.at[i], to)
+        for i, (_, source, slot, to) in enumerate(relay_dests)
+    ]
+
+    def arrived(slot, c):
+        remote(
+            edge if c == nc - 1 else own.at[pl.ds(*chunks[c])],
+            partner_edge.at[slot] if c == nc - 1 else partner.at[slot, pl.ds(*chunks[c])],
+            own_send.at[0, c], item_recv.at[slot, c], date, rng,
+        ).wait_recv()
+
+    def send_own(c, which):
+        for i in which:
+            @pl.when(own_dests[i][0])
+            def _(i=i):
+                own_copies[i][c].start()
 
     def store_own(s, keep=None):
         if s < TILES:
@@ -316,11 +357,12 @@
         tile = resample_tile(s, samples, first, second, lane, diff)
         if keep is not None:
             tile = jnp.where(keep, tile, 0.0)
-        own[s] = tile.astype(BF16).reshape(2, ROWS, LANES)
+            edge[...] = pack_edge(tile, lane).astype(BF16)
+        own[at(s)] = tile.astype(BF16).reshape(2, ROWS, LANES)
 
     for s in range(1, 7):
         store_own(s)
-    send_own(0)
+    send_own(0, (0, 1, 2))
 
     @pl.when(has_right)
     def _():
@@ -338,9 +380,9 @@
     high_edge = jnp.where(has_left, 64, 128)
     store_own(7)
     store_own(8, jnp.logical_or(lane < low_edge, lane >= high_edge))
-    send_own(1)
     store_own(0)
-    send_own(2)
+    send_own(1, (0, 1, 2))
+    send_own(2, (0, 1, 2))
 
     for copy in scatters:
         copy.wait_recv()
@@ -360,24 +402,26 @@
     for p in range(TILES):
         own_spec[p] = parts[p]
 
-    def relay(c):
-        @pl.when(has_after)
+    def relay(source, c):
+        exists = {0: y + 1 < NY, 2: jnp.logical_and(has_after, y >= 1), 3: has_after}[source]
+
+        @pl.when(exists)
         def _():
-            own_copies[0][c].wait_recv()
-
-        for (present, _, _), copies in zip(relay_dests, relay_copies):
-            @pl.when(present)
-            def _(copies=copies):
-                copies[c].start()
-
-    relay(0)
+            arrived(source, c)
+
+        for (present, at_slot, _, _), copies in zip(relay_dests, relay_copies):
+            if at_slot == source:
+                @pl.when(present)
+                def _(copies=copies):
+                    copies[c].start()
+
+    relay(0, 0)
+    relay(3, 0)
 
     for s in range(9):
-        real, imag = own[s, 0].astype(F32), own[s, 1].astype(F32)
+        real, imag = own[at(s), 0].astype(F32), own[at(s), 1].astype(F32)
         fields[s, 0:64] = (real * real + imag * imag).astype(BF16)
-    lines = table[LINES : LINES + 192, 0:192]
-    for g in range(4):
-        box_own[:, 256 * g : 256 * g + 256] = box_group(g, fields, 64, table, table[LINES : LINES + 64, 0:64])
+    box_own[...] = boxes(fields, 64, table)
 
     for copy in exchanges:
         copy.wait_recv()
@@ -392,48 +436,61 @@
     for copy in gathers:
         copy.start()
 
-    relay(1)
-    relay(2)
+    for c in range(1, nc):
+        relay(0, c)
+        relay(3, c)
 
     def pair(h):
         slot = h - 1
-        if h < SPAN:
-            for c in range(nc):
-                own_copies[h][c].wait_recv()
+        partner[slot, TILES] = unpack_edge(partner_edge[slot].astype(F32), lane).astype(BF16).reshape(2, ROWS, LANES)
         for s in range(9):
-            own0, own1 = own[s, 0].astype(F32), own[s, 1].astype(F32)
-            other0, other1 = partner[slot, s, 0].astype(F32), partner[slot, s, 1].astype(F32)
+            own0, own1 = own[at(s), 0].astype(F32), own[at(s), 1].astype(F32)
+            other0, other1 = partner[slot, at(s), 0].astype(F32), partner[slot, at(s), 1].astype(F32)
             fields[s, 0:64] = (own0 * other0 + own1 * other1).astype(BF16)
             fields[s, 64:128] = (own1 * other0 - own0 * other1).astype(BF16)
             fields[s, 128:192] = (other0 * other0 + other1 * other1).astype(BF16)
         weight = part_s[0, slot].astype(F32)
-        for g in range(4):
-            box = box_group(g, fields, 192, table, lines)
-            re, im, power = box[0:64], box[64:128], box[128:192]
-            mine = box_own[:, 256 * g : 256 * g + 256]
-            value = weight * (re * re + im * im) / (mine * power + 1e-06)
-            coh[slot, :, 256 * g : 256 * g + 256] = value.astype(BF16)
+        box = boxes(fields, 192, table)
+        re, im, power = box[0:64], box[64:128], box[128:192]
+        coh[slot] = (weight * (re * re + im * im) / (box_own[...] * power + 1e-06)).astype(BF16)
 
     @pl.when(has_after)
     def _():
         pair(SPAN)
 
-    for h in range(1, NY):
-        @pl.when(y + h < NY)
-        def _(h=h):
-            pair(h)
+    @pl.when(y + 1 < NY)
+    def _():
+        pair(1)
+
+    for c in range(nc):
+        relay(2, c)
+
+    @pl.when(y + 3 < NY)
+    def _():
+        for c in range(nc):
+            arrived(2, c)
+        pair(3)
+
+    @pl.when(jnp.logical_and(has_after, y >= 1))
+    def _():
+        pair(3)
 
     for copy in gathers:
         copy.wait_recv()
     ref_parts, ref_energy = spectrum(ref_amp, table, lane8)
     surfaces(own_spec, own_energy, ref_parts, ref_energy, table, surf, lane8)
 
-    for h in range(1, NY):
-        @pl.when(y + h >= NY)
-        def _(h=h):
-            @pl.when(has_after)
-            def _():
-                pair(h)
+    @pl.when(jnp.logical_or(y + 2 < NY, has_after))
+    def _():
+        for c in range(nc):
+            arrived(1, c)
+        pair(2)
+
+    @pl.when(jnp.logical_and(has_after, y + 1 >= NY))
+    def _():
+        for c in range(nc):
+            arrived(0, c)
+        pair(1)
 
     for copy in scatters + exchanges + gathers:
         copy.wait_send()
@@ -449,7 +506,7 @@
             copy.wait_send()
 
     for dests, copies in ((own_dests, own_copies), (relay_dests, relay_copies)):
-        for (present, _, _), mine in zip(dests, copies):
+        for (present, *_), mine in zip(dests, copies):
             @pl.when(present)
             def _(mine=mine):
                 for copy in mine:
@@ -498,7 +555,9 @@
             pltpu.VMEM(slab, BF16),
             pltpu.VMEM((TILES, 128, LANES), F32),
             pltpu.VMEM((9,) + tile, BF16),
+            pltpu.VMEM((32, LANES), BF16),
             pltpu.VMEM((SPAN, 9) + tile, BF16),
+            pltpu.VMEM((SPAN, 32, LANES), BF16),
             pltpu.VMEM((9, 192, LANES), BF16),
             pltpu.VMEM((ROWS, TILES * LANES), F32),
             dma((TILES + 1,)),
@@ -506,7 +565,7 @@
             dma((max(nz - 1, 1),)), dma((max(nz - 1, 1),)),
             dma((nxy - 1,)), dma((nxy - 1,)),
             dma((max(nz - 1, 1),)), dma((max(nz - 1, 1),)),
-            dma((4, 3)), dma((3, 3)), dma((4, 3)),
+            dma((3, 3)), dma((4, 3)), dma((4, 3)),
         ],
         compiler_params=pltpu.CompilerParams(collective_id=0, has_side_effects=True),
     )(ref_date, int_offset, frac_offset, partners, slc, tables())

time: 38 us -> 34.1 us (0.90)
  the two profiles are of different devices: /device:TPU:8 before, /device:TPU:24 now
where the time goes in v3:
time: 34.1 us; the launch traced here: 34 us
  Pallas kernels  32.7 us (96%)
  between operations  1.28 us (4%)
    pallas_call x1, Pallas kernels, body(): pl.pallas_call(functools.partial(kernel, nz, nx, nr), out_shape=(pltpu.VM...  31.9 us
    pallas_call x1, Pallas kernels, body(): pl.pallas_call(write_kernel, out_shape=(jax.ShapeDtypeStruct((1, 1, 16, 1...  0.82 us

profile of v3, /device:TPU:24, one launch (start us, length us, event | category | flops | bytes accessed | tf_op | source)
XLA Modules:
  0.0 34.0 jit_solution(4505464423001507402)
XLA Ops:
  1.3 31.9 %shard_map.77 = (f32[16,8,128]{2,1,0:T(8,128)S(1)}, bf16[4,64,1024]{2,1,0:T(8,128)(2,1)S(1)}) custom-call(s32[1]{0:T(128)S(6)} %copy.8.ref_s, s32[1,1,16]{2,1,0:T(1,128)} %off_s.1, f32[1,1,16]{2,1,0:T(1,128)} %frac_s.1, s32[1,4]{1,0:T(1,128)} %part_s.1, bf16[1,2,64,1024]{3,2,1,0:T(8,128)(2,1)} %slc_h.1, bf16[1248,256]{1,0:T(8,128)(2,1)} %constant.2.clone.table_h), custom_call_target="tpu_custom_call" | custom-call | tf_op jit(solution)/shard_map/pallas_call | solution.py:536
  33.1 0.8 %shard_map.78 = (f32[1,1,16,1024]{3,2,1,0:T(8,128)}, bf16[1,4,64,1024]{3,2,1,0:T(8,128)(2,1)}) custom-call(f32[16,8,128]{2,1,0:T(8,128)S(1)} %get-tuple-element.4.surf, bf16[4,64,1024]{2,1,0:T(8,128)(2,1)S(1)} %get-tuple-element.5.coh), custom_call_target="tpu_custom_call" | custom-call | tf_op jit(solution)/shard_map/pallas_call | solution.py:572

commit v4 on v3

--- a/solution.py
+++ b/solution.py
@@ -188,12 +188,12 @@
 
 def kernel(
     nz, nx, nr,
-    ref_s, off_s, frac_s, part_s, slc_h, table_h,
+    ref_h, off_h, frac_h, part_h, slc_h, table_h,
     surf, coh,
     table, samples, halo, taps, tap_halo, amp, masked, scatter, merged, exchange, ref_amp,
     own_spec, own, edge, partner, partner_edge, fields, box_own,
     in_sem, halo_send, halo_recv, rs_send, rs_recv, ae_send, ae_recv, ag_send, ag_recv,
-    own_send, relay_send, item_recv,
+    own_send, relay_send, item_recv, scalar_sem, ref_s, off_s, frac_s, part_s,
 ):
     date, rng = lax.axis_index("date"), lax.axis_index("rng")
     planes = nx * nz
@@ -216,15 +216,6 @@
             src_ref=src, dst_ref=dst, send_sem=send, recv_sem=recv,
             device_id=(to_date, to_rng), device_id_type=MESH,
         )
-
-    loads = [
-        pltpu.make_async_copy(slc_h.at[0, :, :, pl.ds(128 * p, 128)], samples.at[p], in_sem.at[p])
-        for p in range(TILES)
-    ]
-    for load in loads:
-        load.start()
-    table_load = pltpu.make_async_copy(table_h, table, in_sem.at[TILES])
-    table_load.start()
 
     barrier = pltpu.get_barrier_semaphore()
 
@@ -243,9 +234,26 @@
         def _(to_date=to_date, to_rng=to_rng):
             hello(to_date, to_rng)
 
+    loads = [
+        pltpu.make_async_copy(slc_h.at[0, :, :, pl.ds(128 * p, 128)], samples.at[p], in_sem.at[p])
+        for p in range(TILES)
+    ]
+    for load in loads:
+        load.start()
+    table_load = pltpu.make_async_copy(table_h, table, in_sem.at[TILES])
+    table_load.start()
+    scalars = [
+        pltpu.make_async_copy(source, target, scalar_sem.at[i])
+        for i, (source, target) in enumerate(((off_h, off_s), (frac_h, frac_s), (part_h, part_s), (ref_h, ref_s)))
+    ]
+    for copy in scalars:
+        copy.start()
+
     lane = lax.broadcasted_iota(jnp.int32, (LANES, LANES), 1)
     diff = lax.broadcasted_iota(jnp.int32, (LANES, LANES), 0) - lane
     lane8 = lane[0:8]
+    for copy in scalars:
+        copy.wait()
     rows = tap_rows(off_s, frac_s)
     taps[...] = rows
 
@@ -293,6 +301,9 @@
         remote(taps.at[pl.ds(8, 8)], tap_halo.at[0], halo_send.at[3], halo_recv.at[3], date, rng + 1),
     ]
 
+    for copy in scatters:
+        copy.start()
+
     @pl.when(has_left)
     def _():
         for copy in to_left:
@@ -303,10 +314,7 @@
         for copy in to_right:
             copy.start()
 
-    for copy in scatters:
-        copy.start()
-
-    chunks = ((2, 6), (0, 2))
+    chunks = ((2, 3), (5, 3), (0, 2))
     nc = len(chunks) + 1
 
     def item_copies(source, source_edge, slot, sends, to_date):
@@ -360,9 +368,12 @@
             edge[...] = pack_edge(tile, lane).astype(BF16)
         own[at(s)] = tile.astype(BF16).reshape(2, ROWS, LANES)
 
-    for s in range(1, 7):
+    for s in range(1, 4):
         store_own(s)
     send_own(0, (0, 1, 2))
+    for s in range(4, 7):
+        store_own(s)
+    send_own(1, (0, 1, 2))
 
     @pl.when(has_right)
     def _():
@@ -381,8 +392,8 @@
     store_own(7)
     store_own(8, jnp.logical_or(lane < low_edge, lane >= high_edge))
     store_own(0)
-    send_own(1, (0, 1, 2))
     send_own(2, (0, 1, 2))
+    send_own(3, (0, 1, 2))
 
     for copy in scatters:
         copy.wait_recv()
@@ -415,8 +426,9 @@
                 def _(copies=copies):
                     copies[c].start()
 
-    relay(0, 0)
-    relay(3, 0)
+    for c in range(2):
+        relay(0, c)
+        relay(3, c)
 
     for s in range(9):
         real, imag = own[at(s), 0].astype(F32), own[at(s), 1].astype(F32)
@@ -436,9 +448,11 @@
     for copy in gathers:
         copy.start()
 
-    for c in range(1, nc):
+    for c in range(2, nc):
         relay(0, c)
         relay(3, c)
+    for c in range(2):
+        relay(2, c)
 
     def pair(h):
         slot = h - 1
@@ -462,7 +476,7 @@
     def _():
         pair(1)
 
-    for c in range(nc):
+    for c in range(2, nc):
         relay(2, c)
 
     @pl.when(y + 3 < NY)
@@ -474,6 +488,12 @@
     @pl.when(jnp.logical_and(has_after, y >= 1))
     def _():
         pair(3)
+
+    @pl.when(jnp.logical_and(has_after, y + 1 >= NY))
+    def _():
+        for c in range(nc):
+            arrived(0, c)
+        pair(1)
 
     for copy in gathers:
         copy.wait_recv()
@@ -485,12 +505,6 @@
         for c in range(nc):
             arrived(1, c)
         pair(2)
-
-    @pl.when(jnp.logical_and(has_after, y + 1 >= NY))
-    def _():
-        for c in range(nc):
-            arrived(0, c)
-        pair(1)
 
     for copy in scatters + exchanges + gathers:
         copy.wait_send()
@@ -527,7 +541,6 @@
 def body(nz, nx, nr, slc, ref_date, int_offset, frac_offset, partners):
     ts = TILES // nz
     nxy = nx * NY
-    smem = pl.BlockSpec(memory_space=pltpu.SMEM)
     anywhere = pl.BlockSpec(memory_space=pl.ANY)
     vmem = pl.BlockSpec(memory_space=pltpu.VMEM)
     dma = pltpu.SemaphoreType.DMA
@@ -539,7 +552,7 @@
             pltpu.VMEM((16, 8, LANES), F32),
             pltpu.VMEM((SPAN, ROWS, TILES * LANES), BF16),
         ),
-        in_specs=[smem, smem, smem, smem, anywhere, anywhere],
+        in_specs=[anywhere] * 6,
         out_specs=(vmem, vmem),
         scratch_shapes=[
             pltpu.VMEM((TABLE_ROWS, 256), BF16),
@@ -565,7 +578,9 @@
             dma((max(nz - 1, 1),)), dma((max(nz - 1, 1),)),
             dma((nxy - 1,)), dma((nxy - 1,)),
             dma((max(nz - 1, 1),)), dma((max(nz - 1, 1),)),
-            dma((3, 3)), dma((4, 3)), dma((4, 3)),
+            dma((3, 4)), dma((4, 4)), dma((4, 4)), dma((4,)),
+            pltpu.SMEM((1,), jnp.int32), pltpu.SMEM((1, 1, 16), jnp.int32),
+            pltpu.SMEM((1, 1, 16), F32), pltpu.SMEM((1, SPAN), jnp.int32),
         ],
         compiler_params=pltpu.CompilerParams(collective_id=0, has_side_effects=True),
     )(ref_date, int_offset, frac_offset, partners, slc, tables())

time: 34.1 us -> 32.5 us (0.953)
  the two profiles are of different devices: /device:TPU:24 before, /device:TPU:16 now
where the time goes in v4:
time: 32.5 us; the launch traced here: 32.4 us
  Pallas kernels  31.1 us (96%)
  between operations  1.28 us (4%)
    pallas_call x1, Pallas kernels, body(): pl.pallas_call(functools.partial(kernel, nz, nx, nr), out_shape=(pltpu.VM...  30.3 us
    pallas_call x1, Pallas kernels, body(): pl.pallas_call(write_kernel, out_shape=(jax.ShapeDtypeStruct((1, 1, 16, 1...  0.82 us

profile of v4, /device:TPU:16, one launch (start us, length us, event | category | flops | bytes accessed | tf_op | source)
XLA Modules:
  0.0 32.4 jit_solution(7623501794526921216)
XLA Ops:
  1.3 30.3 %shard_map.77 = (f32[16,8,128]{2,1,0:T(8,128)S(1)}, bf16[4,64,1024]{2,1,0:T(8,128)(2,1)S(1)}) custom-call(s32[1]{0:T(128)S(6)} %copy.8.ref_h, s32[1,1,16]{2,1,0:T(1,128)} %off_h.1, f32[1,1,16]{2,1,0:T(1,128)} %frac_h.1, s32[1,4]{1,0:T(1,128)} %part_h.1, bf16[1,2,64,1024]{3,2,1,0:T(8,128)(2,1)} %slc_h.1, bf16[1248,256]{1,0:T(8,128)(2,1)} %constant.2.clone.table_h), custom_call_target="tpu_custom_call" | custom-call | tf_op jit(solution)/shard_map/pallas_call | solution.py:549
  31.6 0.8 %shard_map.78 = (f32[1,1,16,1024]{3,2,1,0:T(8,128)}, bf16[1,4,64,1024]{3,2,1,0:T(8,128)(2,1)}) custom-call(f32[16,8,128]{2,1,0:T(8,128)S(1)} %get-tuple-element.4.surf, bf16[4,64,1024]{2,1,0:T(8,128)(2,1)S(1)} %get-tuple-element.5.coh), custom_call_target="tpu_custom_call" | custom-call | tf_op jit(solution)/shard_map/pallas_call | solution.py:587
